TPU v7x, 512 devices: a whole 4x8x8 slice. The times are simulated.
512 devices in a mesh: river: 16 (over y_hi, x, core), hours: 32 (over y_lo, z).
Axes of the slice: x: 4, y: 8 (y_hi: 2, y_lo: 4; y = y_hi * 4 + y_lo), z: 8, core: 2. Of those that a mesh axis runs over, the one named last changes fastest.
Arguments:
- release: float32 [160, 512, 512], P('river', 'hours'), may hold values from 0 to 1
- storage_dual: float32 [160, 512, 512], P('river', 'hours'), may hold values from -3 to 3
- demand_dual: float32 [512, 512], P('hours'), may hold values from -1 to 0
- cost: float32 [160, 512, 512], P('river', 'hours'), may hold values from -1.8 to 1.8
- inflow: float32 [160, 512, 512], P('river', 'hours'), may hold values from 0 to 1.2
- demand: float32 [512, 512], P('hours'), may hold values from 4.427189 to 8.221922
- storage_start: float32 [160], P('river'), may hold values from -0.5 to 0.5
- storage_low: float32 [160], P('river'), may hold values from -2 to -0.5
- storage_high: float32 [160], P('river'), may hold values from 0.5 to 2
- release_cap: float32 [160], P('river'), may hold values from 0.5 to 1.5
- efficiency: float32 [160], P('river'), may hold values from 0.5 to 1.5
- downstream: int32 [160], P('river'), may hold values from -1 to 159, as said below
- travel_delay: int32 [160], P('river'), may hold values from 1 to 6
Outputs:
- release_new: float32 [160, 512, 512], P('river', 'hours')
- storage_dual_new: float32 [160, 512, 512], P('river', 'hours')
- demand_dual_new: float32 [512, 512], P('hours')
- storage_excess: float32 [160, 512, 512], P('river', 'hours')
Inputs may be any that keep to these rules, and one draw needn't show every extreme that they name: Each reservoir's downstream index is -1 or lies 1 to 10 positions after its own index.
All inputs are finite; a program needn't handle non-finite values.
Results may differ from a plain program's by a relative error of at most 0.00013.
Values sent between devices are 32-bit elements; how exact they have to be, the bound alone decides.
A program may use at most 64 MiB of HBM per device.

v0:
```python
import math
import jax
import jax.numpy as jnp
from jax import lax
from jax.sharding import PartitionSpec as P

DMAX = 6
primal_step = 1.0
dual_step = 0.1


def passed_along(block, axis, distance):
    devices = range(lax.axis_size(axis))
    route = [(i - distance, i) for i in devices if i - distance in devices]
    return lax.ppermute(block, axis, route)


def prefix(part, axis, combine, identity, reverse):
    count = lax.axis_size(axis)
    place = lax.axis_index(axis)
    ahead = count - 1 - place if reverse else place
    gathered = lax.all_gather(part, axis)
    state = jnp.zeros_like(part) + jnp.asarray(identity, part.dtype)

    def one(turn, state):
        source = count - 1 - turn if reverse else turn
        return combine(state, lax.dynamic_index_in_dim(gathered, source, 0, False))

    return lax.fori_loop(0, ahead, one, state)


def add_pair(earlier_part, later_part):
    return earlier_part + later_part


def hold_back(field, travel_delay, earlier_rim):
    length = field.shape[1]
    extended = jnp.concatenate([earlier_rim, field], 1)
    result = jnp.zeros_like(field)
    for lag_hours in range(1, DMAX + 1):
        window = extended[:, DMAX - lag_hours : DMAX - lag_hours + length]
        result = result + jnp.where((travel_delay == lag_hours)[:, None, None], window, 0.0)
    return result


def bring_forward(field, travel_delay, later_rim):
    length = field.shape[1]
    extended = jnp.concatenate([field, later_rim], 1)
    result = jnp.zeros_like(field)
    for lag_hours in range(1, DMAX + 1):
        window = extended[:, lag_hours : lag_hours + length]
        result = result + jnp.where((travel_delay == lag_hours)[:, None, None], window, 0.0)
    return result


def route_down(matrix, field):
    return jnp.einsum("ij,jtw->itw", matrix, field, precision=lax.Precision.HIGHEST)


def route_up(matrix, field):
    return jnp.einsum("ij,itw->jtw", matrix, field, precision=lax.Precision.HIGHEST)


def iterate(fields, statics, scales, prefix_sum, suffix_sum, from_earlier, from_later):
    release, storage_dual, demand_dual, cost, inflow, demand = fields
    (
        storage_start,
        storage_low,
        storage_high,
        release_cap,
        efficiency,
        travel_delay,
        to_own,
        to_next,
    ) = statics
    scale_time, scale_sum = scales
    suffix = suffix_sum(storage_dual)
    beyond = passed_along(suffix, "river", -1)
    at_sink = route_up(to_own, suffix) + route_up(to_next, beyond)
    later_duals = bring_forward(at_sink, travel_delay, from_later(at_sink[:, :DMAX]))
    gradient = (
        cost
        + scale_time * (later_duals - suffix)
        + scale_sum * efficiency[:, None, None] * demand_dual[None]
    )
    release_new = jnp.clip(release - primal_step * gradient, 0.0, release_cap[:, None, None])
    extrapolated = 2.0 * release_new - release
    length = extrapolated.shape[1]
    delayed = hold_back(extrapolated, travel_delay, from_earlier(extrapolated[:, length - DMAX :]))
    incoming = passed_along(route_down(to_next, delayed), "river", 1)
    routed = route_down(to_own, delayed) + incoming
    storage = storage_start[:, None, None] + scale_time * prefix_sum(inflow + routed - extrapolated)
    lower_bound = storage_low[:, None, None]
    upper_bound = storage_high[:, None, None]
    storage_dual_new = (
        storage_dual
        + dual_step * storage
        - dual_step * jnp.clip(storage_dual / dual_step + storage, lower_bound, upper_bound)
    )
    storage_excess = storage - jnp.clip(storage, lower_bound, upper_bound)
    partial_power = jnp.sum(scale_sum * efficiency[:, None, None] * extrapolated, 0)
    supplied = lax.psum(partial_power, "river")
    demand_dual_new = jnp.minimum(demand_dual + dual_step * (supplied - demand), 0.0)
    return (release_new, storage_dual_new, demand_dual_new, storage_excess)


def suffix_local(field):
    return jnp.flip(jnp.cumsum(jnp.flip(field, 1), 1), 1)


def shards(
    release,
    storage_dual,
    demand_dual,
    cost,
    inflow,
    demand,
    storage_start,
    storage_low,
    storage_high,
    release_cap,
    efficiency,
    downstream,
    travel_delay,
):
    res_dev = release.shape[0]
    scale_time = 1.0 / (release.shape[1] * lax.axis_size("hours"))
    scale_sum = 1.0 / math.sqrt(res_dev * lax.axis_size("river"))
    base_index = lax.axis_index("river") * res_dev
    target = downstream - base_index
    indices = jnp.arange(res_dev, dtype=jnp.int32)
    to_own = (target[None, :] == indices[:, None]).astype(jnp.float32)
    to_next = (target[None, :] == indices[:, None] + res_dev).astype(jnp.float32)
    statics = (
        storage_start,
        storage_low,
        storage_high,
        release_cap,
        efficiency,
        travel_delay,
        to_own,
        to_next,
    )
    scales = (scale_time, scale_sum)

    def prefix_blocks(field):
        local_sum = jnp.cumsum(field, 1)
        totals = local_sum[:, -1]
        offset = prefix(totals, "hours", add_pair, jnp.zeros_like(totals), False)
        return local_sum + offset[:, None]

    def suffix_blocks(field):
        local_sum = suffix_local(field)
        totals = local_sum[:, 0]
        offset = prefix(totals, "hours", add_pair, jnp.zeros_like(totals), True)
        return local_sum + offset[:, None]

    def earlier_block(part):
        return passed_along(part, "hours", 1)

    def later_block(part):
        return passed_along(part, "hours", -1)

    fields = (release, storage_dual, demand_dual, cost, inflow, demand)
    return iterate(
        fields, statics, scales, prefix_blocks, suffix_blocks, earlier_block, later_block
    )


def solution(mesh):
    return jax.shard_map(
        shards,
        mesh=mesh,
        in_specs=(
            P("river", "hours", None),
            P("river", "hours", None),
            P("hours", None),
            P("river", "hours", None),
            P("river", "hours", None),
            P("hours", None),
            P("river"),
            P("river"),
            P("river"),
            P("river"),
            P("river"),
            P("river"),
            P("river"),
        ),
        out_specs=(
            P("river", "hours", None),
            P("river", "hours", None),
            P("hours", None),
            P("river", "hours", None),
        ),
        check_vma=False,
    )
```

profile of v0, /device:TPU:32, one launch (start us, length us, event | category | flops | bytes accessed | tf_op | source)
XLA Modules:
  0.0 301.1 jit_solution(5361114669511193955)
XLA Ops:
  0.6 1.8 rev.7
  2.5 0.4 fusion.45
  2.9 86.1 %all-gather = f32[320,1,512]{2,1,0:T(1,128)S(1)} all-gather(f32[10,1,512]{2,1,0:T(1,128)S(1)} %copy.42), channel_id=2, replica_groups=mesh['river'=16,'hours'=32] {'hours'}, dimensions={0}, use_global_device_ids=true | all-gather | bytes 675840 | tf_op jit(solution)/shard_map/all_gather | solution.py:22
  89.0 1.6 reduce
  90.5 0.1 reshape.29
  90.7 1.2 while.22
  91.9 1.9 collective-permute-start
  93.8 0.0 copy-start.7
  93.8 0.6 copy-done.7
  94.5 0.6 copy-done.8
  95.2 0.4 fusion.49
  95.6 4.9 %collective-permute-done = f32[10,16,512]{2,0,1:T(8,128)S(1)} collective-permute-done((f32[10,16,512]{2,0,1:T(8,128)S(1)}, f32[10,16,512]{2,0,1:T(8,128)S(1)}, u32[]{:S(2)}, u32[]{:S(2)}) %collective-permute-start) | collective-permute-done | bytes 327712 | tf_op jit(solution)/shard_map/ppermute | solution.py:15
  100.5 0.5 convolution_add_fusion.1
  101.0 0.0 copy-start.12
  101.0 0.0 copy-start.2
  101.0 0.0 copy-start.4
  101.1 1.4 collective-permute-start.1
  102.5 0.0 copy-done.12
  102.5 7.7 %collective-permute-done.1 = f32[10,6,512]{2,0,1:T(8,128)S(1)} collective-permute-done((f32[10,6,512]{2,0,1:T(8,128)S(1)}, f32[10,6,512]{2,0,1:T(8,128)S(1)}, u32[]{:S(2)}, u32[]{:S(2)}) %collective-permute-start.1) | collective-permute-done | bytes 122912 | tf_op jit(solution)/shard_map/ppermute | solution.py:15
  110.2 0.0 copy-done.3
  110.2 0.0 copy-done.2
  110.2 0.0 copy-done.4
  110.2 0.6 copy-done.6
  110.9 0.8 multiply_reduce_fusion
  111.6 1.5 collective-permute-start.2
  113.1 5.1 %collective-permute-done.2 = f32[10,6,512]{2,0,1:T(8,128)S(1)} collective-permute-done((f32[10,6,512]{2,0,1:T(8,128)S(1)}, f32[10,6,512]{2,0,1:T(8,128)S(1)}, u32[]{:S(2)}, u32[]{:S(2)}) %collective-permute-start.2) | collective-permute-done | bytes 122912 | tf_op jit(solution)/shard_map/ppermute | solution.py:15
  118.2 0.3 fusion.12
  118.5 0.4 fusion.51
  118.9 1.9 collective-permute-start.3
  120.8 0.0 copy-start.1
  120.8 0.9 copy.52
  121.7 91.9 %psum.7 = f32[16,512]{1,0:T(8,128)S(1)} all-reduce(f32[16,512]{1,0:T(8,128)S(1)} %get-tuple-element.113), channel_id=1, replica_groups=mesh['river'=16,'hours'=32] {'river'}, use_global_device_ids=true, to_apply=%region_7.8 | all-reduce | flops 8192 | bytes 65536 | tf_op jit(solution)/shard_map/psum | solution.py:102
  213.7 0.0 copy-done.5
  213.7 0.6 add_minimum_fusion
  214.3 0.0 collective-permute-done.3
  214.3 0.5 fusion.1
  214.8 2.7 fusion.63
  217.6 78.7 %all-gather.1 = f32[320,1,512]{2,1,0:T(1,128)S(1)} all-gather(f32[10,1,512]{2,1,0:T(1,128)S(1)} %copy.49), channel_id=3, replica_groups=mesh['river'=16,'hours'=32] {'hours'}, dimensions={0}, use_global_device_ids=true | all-gather | bytes 675840 | tf_op jit(solution)/shard_map/all_gather | solution.py:22
  296.3 1.6 reduce.1
  297.9 0.0 copy-start
  297.9 0.1 reshape.30
  298.0 0.0 copy-start.9
  298.0 0.0 copy-start.10
  298.0 0.0 copy-start.11
  298.0 0.8 copy-done
  298.8 0.4 minimum_subtract_fusion
  299.2 0.9 copy.54
  300.1 0.9 copy.53
  (52 shorter events, 0.5 us)
Async XLA Ops:
  91.9 8.6 %collective-permute-start = (f32[10,16,512]{2,0,1:T(8,128)S(1)}, f32[10,16,512]{2,0,1:T(8,128)S(1)}, u32[]{:S(2)}, u32[]{:S(2)}) collective-permute-start(f32[10,16,512]{2,0,1:T(8,128)S(1)} %reverse_add_fusion), channel_id=1, source_target_pairs={{32,0},{64,32},{96,64},{128,96},{160,128},{192,160},{224,192},{256... | collective-permute-start | bytes 983048 | tf_op jit(solution)/shard_map/ppermute | solution.py:15
  93.8 0.7 copy-start.7
  94.5 0.7 copy-start.8
  100.5 9.7 %copy-start.3 = (f32[10,16,512]{2,1,0:T(8,128)S(1)}, f32[10,16,512]{2,1,0:T(8,128)}, u32[]{:S(2)}) copy-start(f32[10,16,512]{2,1,0:T(8,128)} %param.20) | copy-start | bytes 983044
  101.0 1.5 copy-start.12
  101.0 9.2 %copy-start.2 = (f32[10,16,512]{2,1,0:T(8,128)S(1)}, f32[10,16,512]{2,1,0:T(8,128)}, u32[]{:S(2)}) copy-start(f32[10,16,512]{2,1,0:T(8,128)} %param.17) | copy-start | bytes 983044
  101.0 9.2 %copy-start.4 = (f32[16,512]{1,0:T(8,128)S(1)}, f32[16,512]{1,0:T(8,128)}, u32[]{:S(2)}) copy-start(f32[16,512]{1,0:T(8,128)} %param.19) | copy-start | bytes 98308
  101.1 9.1 %collective-permute-start.1 = (f32[10,6,512]{2,0,1:T(8,128)S(1)}, f32[10,6,512]{2,0,1:T(8,128)S(1)}, u32[]{:S(2)}, u32[]{:S(2)}) collective-permute-start(f32[10,6,512]{2,0,1:T(8,128)S(1)} %slice.66), channel_id=1, source_target_pairs={{1,0},{2,1},{3,2},{4,3},{5,4},{6,5},{7,6},{8,7},{9,8},{10,9},{11,1... | collective-permute-start | bytes 368648 | tf_op jit(solution)/shard_map/ppermute | solution.py:15
  110.2 0.7 copy-start.6
  111.6 6.5 %collective-permute-start.2 = (f32[10,6,512]{2,0,1:T(8,128)S(1)}, f32[10,6,512]{2,0,1:T(8,128)S(1)}, u32[]{:S(2)}, u32[]{:S(2)}) collective-permute-start(f32[10,6,512]{2,0,1:T(8,128)S(1)} %slice.77), channel_id=1, source_target_pairs={{0,1},{1,2},{2,3},{3,4},{4,5},{5,6},{6,7},{7,8},{8,9},{9,10},{10,1... | collective-permute-start | bytes 368648 | tf_op jit(solution)/shard_map/ppermute | solution.py:15
  118.9 95.4 %collective-permute-start.3 = (f32[10,16,512]{2,0,1:T(8,128)S(1)}, f32[10,16,512]{2,0,1:T(8,128)S(1)}, u32[]{:S(2)}, u32[]{:S(2)}) collective-permute-start(f32[10,16,512]{2,0,1:T(8,128)S(1)} %fusion.51), channel_id=1, source_target_pairs={{0,32},{32,64},{64,96},{96,128},{128,160},{160,192},{192,224},{224... | collective-permute-start | bytes 983048 | tf_op jit(solution)/shard_map/ppermute | solution.py:15
  120.8 93.5 %copy-start.1 = (f32[10,16,512]{2,1,0:T(8,128)S(1)}, f32[10,16,512]{2,1,0:T(8,128)}, u32[]{:S(2)}) copy-start(f32[10,16,512]{2,1,0:T(8,128)} %param.21) | copy-start | bytes 983044
  121.7 91.9 %copy-start.5 = (f32[16,512]{1,0:T(8,128)S(1)}, f32[16,512]{1,0:T(8,128)}, u32[]{:S(2)}) copy-start(f32[16,512]{1,0:T(8,128)} %param.22) | copy-start | bytes 98308
  297.9 1.0 copy-start
  298.0 0.8 copy-start.9
  298.0 0.8 copy-start.10
  298.0 0.8 copy-start.11
where the time goes:
time: 301 us
  blocking collectives  257 us (85%)
  waiting for transfers between devices  17.7 us (6%)
  other arithmetic  8.6 us (3%)
  local copies, waits for them, and re-layouts  7.67 us (3%)
  starting transfers between devices  6.72 us (2%)
    all_gather x2, blocking collectives, prefix(): gathered = lax.all_gather(part, axis)  165 us
    psum x1, blocking collectives, iterate(): supplied = lax.psum(partial_power, 'river')  91.9 us
    ppermute x4, waiting for transfers between devices, passed_along(): return lax.ppermute(block, axis, route)  17.7 us
    ppermute x4, starting transfers between devices, passed_along(): return lax.ppermute(block, axis, route)  6.72 us
  transfers between devices with their start and end apart: 4, of which 3 were waited for; matrix products, arithmetic and copies ran while one was open for 1% of the time, Pallas kernels for 0%

commit v1 on v0

--- a/solution.py
+++ b/solution.py
@@ -1,3 +1,4 @@
+import functools
 import math
 import jax
 import jax.numpy as jnp
@@ -7,6 +8,14 @@
 DMAX = 6
 primal_step = 1.0
 dual_step = 0.1
+
+
+def end_loads(a0, named_axis):
+    upper = jnp.sum(lax.all_gather(a0, named_axis), axis=0)
+    return upper
+
+
+register_rings_on = functools.partial(end_loads, named_axis="river")
 
 
 def passed_along(block, axis, distance):
@@ -99,7 +108,7 @@
     )
     storage_excess = storage - jnp.clip(storage, lower_bound, upper_bound)
     partial_power = jnp.sum(scale_sum * efficiency[:, None, None] * extrapolated, 0)
-    supplied = lax.psum(partial_power, "river")
+    supplied = register_rings_on(partial_power)
     demand_dual_new = jnp.minimum(demand_dual + dual_step * (supplied - demand), 0.0)
     return (release_new, storage_dual_new, demand_dual_new, storage_excess)
 

time: 301 us -> 240 us (0.80)
  blocking collectives: 257 us -> 195 us
    psum x1 -> x0, blocking collectives: 91.9 us -> none  [iterate(): supplied = lax.psum(partial_power, 'river')]
    all_gather x0 -> x1, blocking collectives: none -> 30.2 us  [end_loads(): upper = jnp.sum(lax.all_gather(a0, named_axis), axis=0)]
where the time goes in v1:
time: 240 us
  blocking collectives  195 us (81%)
  waiting for transfers between devices  17.7 us (7%)
  other arithmetic  8.63 us (4%)
  local copies, waits for them, and re-layouts  8.39 us (3%)
  starting transfers between devices  6.72 us (3%)
    all_gather x2, blocking collectives, prefix(): gathered = lax.all_gather(part, axis)  165 us
    all_gather x1, blocking collectives, end_loads(): upper = jnp.sum(lax.all_gather(a0, named_axis), axis=0)  30.2 us
    ppermute x4, waiting for transfers between devices, passed_along(): return lax.ppermute(block, axis, route)  17.7 us
    ppermute x4, starting transfers between devices, passed_along(): return lax.ppermute(block, axis, route)  6.72 us
    unnamed x29, local copies, waits for them, and re-layouts  6.26 us
  transfers between devices with their start and end apart: 4, of which 3 were waited for; matrix products, arithmetic and copies ran while one was open for 1% of the time, Pallas kernels for 0%

profile of v1, /device:TPU:32, one launch (start us, length us, event | category | flops | bytes accessed | tf_op | source)
XLA Modules:
  0.0 239.9 jit_solution(8353780990069071880)
XLA Ops:
  0.6 1.8 rev.7
  2.5 0.4 fusion.45
  2.9 86.1 %all-gather = f32[320,1,512]{2,1,0:T(1,128)S(1)} all-gather(f32[10,1,512]{2,1,0:T(1,128)S(1)} %copy.56), channel_id=2, replica_groups=mesh['river'=16,'hours'=32] {'hours'}, dimensions={0}, use_global_device_ids=true | all-gather | bytes 675840 | tf_op jit(solution)/shard_map/all_gather | solution.py:31
  89.0 1.6 reduce
  90.5 0.1 reshape.29
  90.7 1.2 while.22
  91.9 1.9 collective-permute-start
  93.8 0.0 copy-start.7
  93.8 0.6 copy-done.7
  94.5 0.6 copy-done.8
  95.2 0.4 fusion.49
  95.6 4.9 %collective-permute-done = f32[10,16,512]{2,0,1:T(8,128)S(1)} collective-permute-done((f32[10,16,512]{2,0,1:T(8,128)S(1)}, f32[10,16,512]{2,0,1:T(8,128)S(1)}, u32[]{:S(2)}, u32[]{:S(2)}) %collective-permute-start) | collective-permute-done | bytes 327712 | tf_op jit(solution)/shard_map/ppermute | solution.py:24
  100.5 0.5 convolution_add_fusion.1
  101.0 0.0 copy-start.12
  101.0 0.0 copy-start.2
  101.0 0.0 copy-start.4
  101.1 1.4 collective-permute-start.1
  102.5 0.0 copy-done.12
  102.5 7.7 %collective-permute-done.1 = f32[10,6,512]{2,0,1:T(8,128)S(1)} collective-permute-done((f32[10,6,512]{2,0,1:T(8,128)S(1)}, f32[10,6,512]{2,0,1:T(8,128)S(1)}, u32[]{:S(2)}, u32[]{:S(2)}) %collective-permute-start.1) | collective-permute-done | bytes 122912 | tf_op jit(solution)/shard_map/ppermute | solution.py:24
  110.2 0.0 copy-done.3
  110.2 0.0 copy-done.2
  110.2 0.0 copy-done.4
  110.2 0.6 copy-done.6
  110.9 0.8 multiply_reduce_fusion
  111.6 1.5 collective-permute-start.2
  113.1 5.1 %collective-permute-done.2 = f32[10,6,512]{2,0,1:T(8,128)S(1)} collective-permute-done((f32[10,6,512]{2,0,1:T(8,128)S(1)}, f32[10,6,512]{2,0,1:T(8,128)S(1)}, u32[]{:S(2)}, u32[]{:S(2)}) %collective-permute-start.2) | collective-permute-done | bytes 122912 | tf_op jit(solution)/shard_map/ppermute | solution.py:24
  118.2 0.3 fusion.12
  118.5 0.4 fusion.51
  118.9 1.9 collective-permute-start.3
  120.8 30.2 %all-gather.2 = f32[256,512]{1,0:T(8,128)S(1)} all-gather(f32[16,512]{1,0:T(8,128)S(1)} %get-tuple-element.117), channel_id=4, replica_groups=mesh['river'=16,'hours'=32] {'river'}, dimensions={0}, use_global_device_ids=true | all-gather | bytes 557056 | tf_op jit(solution)/shard_map/all_gather | solution.py:14
  151.0 0.9 copy.66
  151.9 0.7 copy-done.5
  152.7 0.6 add_minimum_fusion
  153.3 0.0 collective-permute-done.3
  153.3 0.5 fusion.1
  153.8 2.7 %fusion.63 = f32[10,16,512]{2,0,1:T(8,128)S(1)} fusion(f32[10,16,512]{2,0,1:T(8,128)S(1)} %fusion.1), kind=kOutput, calls=%fused_computation.105 | output fusion | flops 1228800 | bytes 655360 | tf_op jit(solution)/shard_map/jit(cumsum)/reduce_window_sum | solution.py:156
  156.6 78.6 %all-gather.1 = f32[320,1,512]{2,1,0:T(1,128)S(1)} all-gather(f32[10,1,512]{2,1,0:T(1,128)S(1)} %copy.63), channel_id=3, replica_groups=mesh['river'=16,'hours'=32] {'hours'}, dimensions={0}, use_global_device_ids=true | all-gather | bytes 675840 | tf_op jit(solution)/shard_map/all_gather | solution.py:31
  235.2 1.6 reduce.1
  236.7 0.0 copy-start
  236.8 0.1 reshape.30
  236.9 0.0 copy-start.9
  236.9 0.0 copy-start.10
  236.9 0.0 copy-start.11
  236.9 0.8 copy-done
  237.7 0.0 copy-done.11
  237.7 0.4 minimum_subtract_fusion
  238.1 0.9 copy.68
  239.0 0.9 copy.67
  (53 shorter events, 0.5 us)
Async XLA Ops:
  91.9 8.6 %collective-permute-start = (f32[10,16,512]{2,0,1:T(8,128)S(1)}, f32[10,16,512]{2,0,1:T(8,128)S(1)}, u32[]{:S(2)}, u32[]{:S(2)}) collective-permute-start(f32[10,16,512]{2,0,1:T(8,128)S(1)} %reverse_add_fusion), channel_id=1, source_target_pairs={{32,0},{64,32},{96,64},{128,96},{160,128},{192,160},{224,192},{256... | collective-permute-start | bytes 983048 | tf_op jit(solution)/shard_map/ppermute | solution.py:24
  93.8 0.7 copy-start.7
  94.5 0.7 copy-start.8
  100.5 9.7 %copy-start.3 = (f32[10,16,512]{2,1,0:T(8,128)S(1)}, f32[10,16,512]{2,1,0:T(8,128)}, u32[]{:S(2)}) copy-start(f32[10,16,512]{2,1,0:T(8,128)} %param.20) | copy-start | bytes 983044
  101.0 1.5 copy-start.12
  101.0 9.2 %copy-start.2 = (f32[10,16,512]{2,1,0:T(8,128)S(1)}, f32[10,16,512]{2,1,0:T(8,128)}, u32[]{:S(2)}) copy-start(f32[10,16,512]{2,1,0:T(8,128)} %param.17) | copy-start | bytes 983044
  101.0 9.2 %copy-start.4 = (f32[16,512]{1,0:T(8,128)S(1)}, f32[16,512]{1,0:T(8,128)}, u32[]{:S(2)}) copy-start(f32[16,512]{1,0:T(8,128)} %param.19) | copy-start | bytes 98308
  101.1 9.1 %collective-permute-start.1 = (f32[10,6,512]{2,0,1:T(8,128)S(1)}, f32[10,6,512]{2,0,1:T(8,128)S(1)}, u32[]{:S(2)}, u32[]{:S(2)}) collective-permute-start(f32[10,6,512]{2,0,1:T(8,128)S(1)} %slice.66), channel_id=1, source_target_pairs={{1,0},{2,1},{3,2},{4,3},{5,4},{6,5},{7,6},{8,7},{9,8},{10,9},{11,1... | collective-permute-start | bytes 368648 | tf_op jit(solution)/shard_map/ppermute | solution.py:24
  110.2 0.7 copy-start.6
  111.6 6.5 %collective-permute-start.2 = (f32[10,6,512]{2,0,1:T(8,128)S(1)}, f32[10,6,512]{2,0,1:T(8,128)S(1)}, u32[]{:S(2)}, u32[]{:S(2)}) collective-permute-start(f32[10,6,512]{2,0,1:T(8,128)S(1)} %slice.77), channel_id=1, source_target_pairs={{0,1},{1,2},{2,3},{3,4},{4,5},{5,6},{6,7},{7,8},{8,9},{9,10},{10,1... | collective-permute-start | bytes 368648 | tf_op jit(solution)/shard_map/ppermute | solution.py:24
  118.9 34.4 %collective-permute-start.3 = (f32[10,16,512]{2,0,1:T(8,128)S(1)}, f32[10,16,512]{2,0,1:T(8,128)S(1)}, u32[]{:S(2)}, u32[]{:S(2)}) collective-permute-start(f32[10,16,512]{2,0,1:T(8,128)S(1)} %fusion.51), channel_id=1, source_target_pairs={{0,32},{32,64},{64,96},{96,128},{128,160},{160,192},{192,224},{224... | collective-permute-start | bytes 983048 | tf_op jit(solution)/shard_map/ppermute | solution.py:24
  151.9 0.8 copy-start.5
  151.9 1.4 copy-start.1
  236.7 1.0 copy-start
  236.9 0.8 copy-start.9
  236.9 0.8 copy-start.10
  236.9 0.8 copy-start.11
